TPU v7x, 256 devices: a whole 4x4x8 slice. The times are simulated.
256 devices in a mesh: stream: 2 (over z_hi), dp: 16 (over x, y), tensor: 8 (over z_lo, core).
Axes of the slice: x: 4, y: 4, z: 8 (z_hi: 2, z_lo: 4; z = z_hi * 4 + z_lo), core: 2. Of those that a mesh axis runs over, the one named last changes fastest.
Arguments:
- hidden: bfloat16 [2, 256, 8192], P('stream', 'tensor', 'dp'), may hold values from -3 to 3
- cached_rotated_keys: bfloat16 [2, 256, 8, 256, 128], P('stream', 'dp', 'tensor'), may hold values from -6 to 6
- cached_values: bfloat16 [2, 256, 8, 256, 128], P('stream', 'dp', 'tensor'), may hold values from -18 to 18
- cache_lengths: int32 [2, 256], P('stream', 'dp'), may hold values from 1 to 256, as said below
- recent_ids: int32 [256, 128], replicated, may hold values from 0 to 65535
- guidance: float32 [256], replicated, may hold values from 1 to 3
- w_query: bfloat16 [8192, 8192], P('dp', 'tensor'), may hold values from -0.0625 to 0.0625
- key_value_weight: bfloat16 [8192, 2, 1024], P('dp', None, 'tensor'), may hold values from -0.0625 to 0.0625
- w_output: bfloat16 [8192, 8192], P('tensor', 'dp'), may hold values from -0.0625 to 0.0625
- norm_gain: bfloat16 [8192], P('dp'), may hold values from 0.5 to 1.5
- w_head: bfloat16 [8192, 65536], P(None, ('dp', 'tensor')), may hold values from -0.16503906 to 0.16503906
Outputs:
- guided_logprobs: float32 [256, 65536], P('stream', ('dp', 'tensor'))
Inputs may be any that keep to these rules, and one draw needn't show every extreme that they name: `cache_lengths`: every prompt has 1 to 256 filled slots in each stream; some prompt has all 256; lengths differ widely from one group of 16 prompts to the next.
All inputs are finite; a program needn't handle non-finite values.
Results may differ from a plain program's by a relative error of at most 0.0025.
Values may be sent and summed in bfloat16 or wider, within the bound.
A program may use at most 64 MiB of HBM per device.

v0:
```python
import jax
import jax.numpy as jnp
from jax import lax
from jax.sharding import PartitionSpec as P

MODEL_WIDTH = 8192
HEAD_SIZE = 128
rope_theta = 500000.0
penalty_step = 1.5
norm_eps = 1e-05


def partner_2(value, axis, distance):
    mask = 2**distance
    pairs = [(source, source ^ mask) for source in range(lax.axis_size(axis))]
    return lax.ppermute(value, axis, pairs)


def rotate(values, positions):
    halfway = values.shape[-1] // 2
    frequency = rope_theta ** (-(jnp.arange(halfway, dtype=jnp.float32) * 2.0 / values.shape[-1]))
    angles = positions.astype(jnp.float32)[:, None, None] * frequency
    cosine_term = jnp.cos(angles)
    sine_term = jnp.sin(angles)
    first_half = values[..., :halfway]
    second_half = values[..., halfway:]
    return jnp.concatenate(
        [
            first_half * cosine_term - second_half * sine_term,
            second_half * cosine_term + first_half * sine_term,
        ],
        axis=-1,
    )


def repeat_counts(recent_ids, first_column, width):
    columns = first_column + jnp.arange(width, dtype=jnp.int32)
    return jnp.sum((recent_ids[:, :, None] == columns[None, None, :]).astype(jnp.float32), 1)


def body(
    hidden,
    cached_rotated_keys,
    cached_values,
    cache_lengths,
    recent_ids,
    guidance,
    w_query,
    key_value_weight,
    w_output,
    norm_gain,
    w_head,
):
    local_width = hidden.shape[2]
    query_cols = w_query.shape[1]
    kv_cols = key_value_weight.shape[2]
    local_prompts = cache_lengths.shape[1]
    lengths = cache_lengths[0]
    vocab_local = w_head.shape[1]
    all_rows = lax.all_gather(hidden[0], "tensor", axis=0, tiled=True)
    kv_flat = key_value_weight.reshape(local_width, 2 * kv_cols)
    projected = lax.psum_scatter(
        jnp.concatenate(
            [
                jnp.dot(all_rows, w_query, preferred_element_type=jnp.float32),
                jnp.dot(all_rows, kv_flat, preferred_element_type=jnp.float32),
            ],
            axis=1,
        ),
        "dp",
        scatter_dimension=0,
        tiled=True,
    )
    query_heads = query_cols // HEAD_SIZE
    kv_heads = kv_cols // HEAD_SIZE
    rotated_query = rotate(
        projected[:, :query_cols].reshape(local_prompts, query_heads, HEAD_SIZE), lengths
    ).astype(jnp.bfloat16)
    key_value_rows = projected[:, query_cols:].reshape(local_prompts, 2, kv_heads, HEAD_SIZE)
    fresh_key = rotate(key_value_rows[:, 0], lengths).astype(jnp.bfloat16)
    value_new = key_value_rows[:, 1].astype(jnp.bfloat16)
    grouped_queries = rotated_query.reshape(
        local_prompts, kv_heads, query_heads // kv_heads, HEAD_SIZE
    )
    attention_scale = HEAD_SIZE ** (-0.5)
    key_block = cached_rotated_keys[0]
    value_block = cached_values[0]
    scores = (
        jnp.einsum(
            "pkgd,pksd->pkgs", grouped_queries, key_block, preferred_element_type=jnp.float32
        )
        * attention_scale
    )
    self_score = (
        jnp.einsum("pkgd,pkd->pkg", grouped_queries, fresh_key, preferred_element_type=jnp.float32)
        * attention_scale
    )
    valid = jnp.arange(key_block.shape[2], dtype=jnp.int32)[None, :] < lengths[:, None]
    exps = jnp.where(valid[:, None, None, :], jnp.exp(scores), 0.0)
    own_exp = jnp.exp(self_score)
    denominator = jnp.sum(exps, -1) + own_exp
    weights = (exps / denominator[..., None]).astype(jnp.bfloat16)
    own_weight = (own_exp / denominator).astype(jnp.bfloat16)
    attended = jnp.einsum(
        "pkgs,pksd->pkgd", weights, value_block, preferred_element_type=jnp.float32
    )
    attended = (
        attended
        + own_weight.astype(jnp.float32)[..., None] * value_new.astype(jnp.float32)[:, :, None, :]
    )
    attended = attended.reshape(local_prompts, query_cols).astype(jnp.bfloat16)
    partial_out = jnp.dot(
        lax.all_gather(attended, "dp", axis=0, tiled=True),
        w_output,
        preferred_element_type=jnp.float32,
    )
    output_sum = lax.psum_scatter(partial_out, "tensor", scatter_dimension=0, tiled=True)
    residual = (hidden[0].astype(jnp.float32) + output_sum).astype(jnp.bfloat16)
    widened = residual.astype(jnp.float32)
    squares = lax.psum(jnp.sum(widened * widened, 1), "dp")
    inverse = lax.rsqrt(squares / MODEL_WIDTH + norm_eps)
    normed = (widened * inverse[:, None] * norm_gain.astype(jnp.float32)).astype(jnp.bfloat16)
    normed_all = lax.all_gather(normed, "tensor", axis=0, tiled=True)
    logits = jnp.dot(
        lax.all_gather(normed_all, "dp", axis=1, tiled=True),
        w_head,
        preferred_element_type=jnp.float32,
    )
    stream_side = lax.axis_index("stream")
    half_rows = logits.shape[0] // 2
    mine_start = stream_side * half_rows
    other_start = (1 - stream_side) * half_rows
    column_base = lax.axis_index(("dp", "tensor")) * vocab_local
    mine = lax.dynamic_slice_in_dim(logits, mine_start, half_rows, 0)
    sending = lax.dynamic_slice_in_dim(logits, other_start, half_rows, 0)
    partner = partner_2(sending, "stream", 0)
    conditional = jnp.where(stream_side == 0, mine, partner)
    unconditional = jnp.where(stream_side == 0, partner, mine)
    guide = lax.dynamic_slice_in_dim(guidance, mine_start, half_rows, 0)[:, None]
    recent_mine = lax.dynamic_slice_in_dim(recent_ids, mine_start, half_rows, 0)
    guided = unconditional + guide * (conditional - unconditional)
    guided = guided - penalty_step * repeat_counts(recent_mine, column_base, vocab_local)
    totals = lax.psum(jnp.sum(jnp.exp(guided), 1), ("dp", "tensor"))
    return guided - jnp.log(totals)[:, None]


def solution(mesh):
    return jax.shard_map(
        body,
        mesh=mesh,
        in_specs=(
            P("stream", "tensor", "dp"),
            P("stream", "dp", "tensor", None, None),
            P("stream", "dp", "tensor", None, None),
            P("stream", "dp"),
            P(),
            P(),
            P("dp", "tensor"),
            P("dp", None, "tensor"),
            P("tensor", "dp"),
            P("dp"),
            P(None, ("dp", "tensor")),
        ),
        out_specs=P("stream", ("dp", "tensor")),
        check_vma=False,
    )
```

profile of v0, /device:TPU:128, one launch (start us, length us, event | category | flops | bytes accessed | tf_op | source)
XLA Modules:
  0.0 647.4 jit_solution(1154850240006349418)
XLA Ops:
  6.6 14.5 %all-gather = bf16[1,256,512]{2,1,0:T(8,128)(2,1)S(1)} all-gather(bf16[1,32,512]{2,1,0:T(8,128)(2,1)} %param.11), channel_id=2, replica_groups=mesh['stream'=2,'dp'=16,'tensor'=8] {'tensor'}, dimensions={1}, use_global_device_ids=true | all-gather | bytes 294912 | tf_op jit(solution)/shard_map/all_gather | solution.py:60
  21.1 0.5 fusion.9
  21.6 1.2 fusion.5
  22.8 1.2 pad_maximum_fusion
  24.1 0.7 bitcast_convert_fusion
  24.7 0.7 iota_compare_fusion
  25.4 0.1 multiply_cosine_fusion.1
  25.6 79.2 %reduce-scatter.3.cloned.1.call-done = f32[16,1280]{1,0:T(8,128)} async-done(((f32[256,1280]{1,0:T(8,128)}), f32[16,1280]{1,0:T(8,128)}) %reduce-scatter.3.cloned.1.call-update) | async-done | bytes 81936 | tf_op jit(solution)/shard_map/reduce_scatter | solution.py:62
  104.8 0.7 slice.36
  105.6 0.1 fusion.30
  105.7 0.8 slice_bitcast_fusion
  106.6 0.1 maximum_bitcast_fusion
  106.6 0.1 subtract_convert_fusion
  106.7 0.2 fusion.25
  106.9 1.7 fusion.33
  108.7 0.3 fusion.2
  109.0 23.3 %all_gather.13 = bf16[256,1024]{1,0:T(8,128)(2,1)S(1)} all-gather(bf16[16,1024]{1,0:T(8,128)(2,1)S(1)} %bitcast.51), channel_id=1, replica_groups=mesh['stream'=2,'dp'=16,'tensor'=8] {'dp'}, dimensions={0}, use_global_device_ids=true | all-gather | bytes 557056 | tf_op jit(solution)/shard_map/all_gather | solution.py:113
  132.3 1.2 fusion.34
  133.6 32.9 %reduce-scatter.5.cloned.1.call-done = f32[32,512]{1,0:T(8,128)} async-done(((f32[256,512]{1,0:T(8,128)}), f32[32,512]{1,0:T(8,128)}) %reduce-scatter.5.cloned.1.call-update) | async-done | bytes 65552 | tf_op jit(solution)/shard_map/reduce_scatter | solution.py:117
  166.5 1.0 fusion.11
  167.5 40.3 %psum.14 = f32[32]{0:T(128)S(1)} all-reduce(f32[32]{0:T(128)S(1)} %fusion.11), channel_id=1, replica_groups=mesh['stream'=2,'dp'=16,'tensor'=8] {'dp'}, use_global_device_ids=true, to_apply=%region_4.5 | all-reduce | flops 32 | bytes 256 | tf_op jit(solution)/shard_map/psum | solution.py:120
  207.8 0.9 fusion.13
  208.7 15.3 %all_gather.14 = bf16[256,512]{1,0:T(8,128)(2,1)} all-gather(bf16[32,512]{1,0:T(8,128)(2,1)S(1)} %fusion.13), channel_id=1, replica_groups=mesh['stream'=2,'dp'=16,'tensor'=8] {'tensor'}, dimensions={0}, use_global_device_ids=true | all-gather | bytes 294912 | tf_op jit(solution)/shard_map/all_gather | solution.py:123
  224.1 0.1 dynamic_slice.14
  224.2 58.3 %all-gather.3.cloned.1.call-done = bf16[256,8192]{1,0:T(8,128)(2,1)} async-done(((bf16[256,512]{1,0:T(8,128)(2,1)}), bf16[256,8192]{1,0:T(8,128)(2,1)}) %all-gather.3.cloned.1.call-update) | async-done | bytes 4194320 | tf_op jit(solution)/shard_map/all_gather | solution.py:125
  282.5 7.0 %fusion.35 = f32[256,512]{1,0:T(8,128)S(1)} fusion(bf16[256,8192]{1,0:T(8,128)(2,1)} %all-gather.3.cloned.1.call-done, bf16[8192,512]{1,0:T(8,128)(2,1)} %param.21), kind=kOutput, calls=%fused_computation.66 | convolution fusion | flops 2147483648 | bytes 13107200 | tf_op jit(solution)/shard_map/dot_general | solution.py:124
  289.5 0.3 collective-permute-start
  289.8 4.7 convert_reduce_fusion
  294.4 11.4 %collective-permute-done = f32[128,512]{1,0:T(8,128)S(1)} collective-permute-done((f32[128,512]{1,0:T(8,128)S(1)}, f32[128,512]{1,0:T(8,128)S(1)}, u32[]{:S(2)}, u32[]{:S(2)}) %collective-permute-start) | collective-permute-done | bytes 262176 | tf_op jit(solution)/shard_map/ppermute | solution.py:16
  305.8 0.2 exponential_reduce_fusion
  306.0 334.1 %psum.15 = f32[128]{0:T(128)S(1)} all-reduce(f32[128]{0:T(128)S(1)} %get-tuple-element.5), channel_id=1, replica_groups=mesh['stream'=2,'dp'=16,'tensor'=8] {'dp','tensor'}, use_global_device_ids=true, to_apply=%region_7.8 | all-reduce | flops 128 | bytes 1024 | tf_op jit(solution)/shard_map/psum | solution.py:143
  640.1 0.8 broadcast_subtract_fusion
  (33 shorter events, 0.3 us)
Async XLA Ops:
  6.5 14.6 %copy-start = (bf16[512,1024]{1,0:T(8,128)(2,1)S(1)}, bf16[512,1024]{1,0:T(8,128)(2,1)}, u32[]{:S(2)}) copy-start(bf16[512,1024]{1,0:T(8,128)(2,1)} %param.17) | copy-start | bytes 3145732
  6.5 160.0 %copy-start.3 = (bf16[1,32,512]{2,1,0:T(8,128)(2,1)S(1)}, bf16[1,32,512]{2,1,0:T(8,128)(2,1)}, u32[]{:S(2)}) copy-start(bf16[1,32,512]{2,1,0:T(8,128)(2,1)} %param.11) | copy-start | bytes 98308
  6.5 102.2 %copy-start.1 = (bf16[1,16,1,256,128]{4,3,2,1,0:T(8,128)(2,1)S(1)}, bf16[1,16,1,256,128]{4,3,2,1,0:T(8,128)(2,1)}, u32[]{:S(2)}) copy-start(bf16[1,16,1,256,128]{4,3,2,1,0:T(8,128)(2,1)} %param.13) | copy-start | bytes 3145732
  6.5 125.8 %copy-start.2 = (bf16[1024,512]{1,0:T(8,128)(2,1)S(1)}, bf16[1024,512]{1,0:T(8,128)(2,1)}, u32[]{:S(2)}) copy-start(bf16[1024,512]{1,0:T(8,128)(2,1)} %param.19) | copy-start | bytes 3145732
  6.5 127.1 %copy-start.5 = (bf16[512]{0:T(512)(128)(2,1)S(1)}, bf16[512]{0:T(512)(128)(2,1)}, u32[]{:S(2)}) copy-start(bf16[512]{0:T(512)(128)(2,1)} %param.20) | copy-start | bytes 3076
  6.5 217.5 %copy-start.6 = (f32[256]{0:T(256)S(1)}, f32[256]{0:T(256)}, u32[]{:S(2)}) copy-start(f32[256]{0:T(256)} %param.16) | copy-start | bytes 3076
  6.6 217.6 %copy-start.4 = (s32[256,128]{1,0:T(8,128)S(1)}, s32[256,128]{1,0:T(8,128)}, u32[]{:S(2)}) copy-start(s32[256,128]{1,0:T(8,128)} %param.15) | copy-start | bytes 393220
  6.6 98.2 %reduce-scatter.3.cloned.1.call-start = ((), (), s32[]{:S(2)}) async-start(), calls=%async_computation.2 | async-start | bytes 1392640 | tf_op jit(solution)/shard_map/reduce_scatter | solution.py:62
  24.0 142.5 %reduce-scatter.5.cloned.1.call-start = ((), (), s32[]{:S(2)}) async-start(), calls=%async_computation.3 | async-start | bytes 589824 | tf_op jit(solution)/shard_map/reduce_scatter | solution.py:117
  133.6 148.9 %all-gather.3.cloned.1.call-start = ((), (), s32[]{:S(2)}) async-start(), calls=%async_computation.4 | async-start | bytes 4456448 | tf_op jit(solution)/shard_map/all_gather | solution.py:125
  289.5 16.3 %collective-permute-start = (f32[128,512]{1,0:T(8,128)S(1)}, f32[128,512]{1,0:T(8,128)S(1)}, u32[]{:S(2)}, u32[]{:S(2)}) collective-permute-start(f32[128,512]{1,0:T(8,128)S(1)} %constant_dynamic-slice_fusion.1), channel_id=1, source_target_pairs={{0,128},{128,0},{1,129},{129,1},{2,130},{130,2},{3,131},{131,3},{4... | collective-permute-start | bytes 786440 | tf_op jit(solution)/shard_map/ppermute | solution.py:16
Sparse Core Ops, SparseCore 0:
  24.1 80.6 reduce-scatter.2
  133.7 32.7 reduce-scatter.4
  224.2 58.2 all-gather.2
where the time goes:
time: 648 us; the launch traced here: 647 us
  blocking collectives  427 us (66%)
  waiting for transfers between devices  182 us (28%)
  between operations  13.3 us (2%)
  matrix products  12.1 us (2%)
  other arithmetic  10.5 us (2%)
    psum x1, blocking collectives, body(): totals = lax.psum(jnp.sum(jnp.exp(guided), 1), ('dp', 'tensor'))  334 us
    reduce_scatter x1, waiting for transfers between devices, body(): lax.psum_scatter(jnp.concatenate([jnp.dot(all_rows, w_query, preferred_el...  79.2 us
    all_gather x1, waiting for transfers between devices, body(): lax.all_gather(normed_all, 'dp', axis=1, tiled=True)  58.3 us
    psum x1, blocking collectives, body(): squares = lax.psum(jnp.sum(widened * widened, 1), 'dp')  40.3 us
    reduce_scatter x1, waiting for transfers between devices, body(): lax.psum_scatter(partial_out, 'tensor', scatter_dimension=0, tiled=True)  32.9 us
    all_gather x1, blocking collectives, body(): lax.all_gather(attended, 'dp', axis=0, tiled=True)  23.3 us
    all_gather x1, blocking collectives, body(): normed_all = lax.all_gather(normed, 'tensor', axis=0, tiled=True)  15.3 us
    all_gather x1, blocking collectives, body(): all_rows = lax.all_gather(hidden[0], 'tensor', axis=0, tiled=True)  14.5 us
  transfers between devices with their start and end apart: 4, of which 4 were waited for; matrix products, arithmetic and copies ran while one was open for 1% of the time, Pallas kernels for 0%

commit v1 on v0

--- a/solution.py
+++ b/solution.py
@@ -140,7 +140,7 @@
     recent_mine = lax.dynamic_slice_in_dim(recent_ids, mine_start, half_rows, 0)
     guided = unconditional + guide * (conditional - unconditional)
     guided = guided - penalty_step * repeat_counts(recent_mine, column_base, vocab_local)
-    totals = lax.psum(jnp.sum(jnp.exp(guided), 1), ("dp", "tensor"))
+    totals = lax.psum(lax.psum(jnp.sum(jnp.exp(guided), 1), "tensor"), "dp")
     return guided - jnp.log(totals)[:, None]
 
 

time: 648 us -> 365 us (0.56)
  blocking collectives: 427 us -> 145 us
    psum x1 -> x2, blocking collectives: 334 us -> 51.7 us  [body(): totals = lax.psum(lax.psum(jnp.sum(jnp.exp(guided), 1), 'tensor'), 'dp')]
  transfers between devices with their start and end apart: 4 -> 4, of which waited for: 4 -> 4; matrix products, arithmetic and copies ran while one was open for 1% -> 2% of each run, Pallas kernels for 0% -> 0%
where the time goes in v1:
time: 365 us
  waiting for transfers between devices  182 us (50%)
  blocking collectives  145 us (40%)
  between operations  13.3 us (4%)
  matrix products  12.1 us (3%)
  other arithmetic  10.5 us (3%)
    reduce_scatter x1, waiting for transfers between devices, body(): lax.psum_scatter(jnp.concatenate([jnp.dot(all_rows, w_query, preferred_el...  79.2 us
    all_gather x1, waiting for transfers between devices, body(): lax.all_gather(normed_all, 'dp', axis=1, tiled=True)  58.3 us
    psum x2, blocking collectives, body(): totals = lax.psum(lax.psum(jnp.sum(jnp.exp(guided), 1), 'tensor'), 'dp')  51.7 us
    psum x1, blocking collectives, body(): squares = lax.psum(jnp.sum(widened * widened, 1), 'dp')  40.3 us
    reduce_scatter x1, waiting for transfers between devices, body(): lax.psum_scatter(partial_out, 'tensor', scatter_dimension=0, tiled=True)  32.9 us
    all_gather x1, blocking collectives, body(): lax.all_gather(attended, 'dp', axis=0, tiled=True)  23.3 us
    all_gather x1, blocking collectives, body(): normed_all = lax.all_gather(normed, 'tensor', axis=0, tiled=True)  15.3 us
    all_gather x1, blocking collectives, body(): all_rows = lax.all_gather(hidden[0], 'tensor', axis=0, tiled=True)  14.5 us
  transfers between devices with their start and end apart: 4, of which 4 were waited for; matrix products, arithmetic and copies ran while one was open for 2% of the time, Pallas kernels for 0%

profile of v1, /device:TPU:128, one launch (start us, length us, event | category | flops | bytes accessed | tf_op | source)
XLA Modules:
  0.0 365.1 jit_solution(7004600347445081312)
XLA Ops:
  6.6 14.5 %all-gather = bf16[1,256,512]{2,1,0:T(8,128)(2,1)S(1)} all-gather(bf16[1,32,512]{2,1,0:T(8,128)(2,1)} %param.11), channel_id=2, replica_groups=mesh['stream'=2,'dp'=16,'tensor'=8] {'tensor'}, dimensions={1}, use_global_device_ids=true | all-gather | bytes 294912 | tf_op jit(solution)/shard_map/all_gather | solution.py:60
  21.1 0.5 fusion.9
  21.6 1.2 fusion.5
  22.8 1.2 pad_maximum_fusion
  24.1 0.7 bitcast_convert_fusion
  24.7 0.7 iota_compare_fusion
  25.4 0.1 multiply_cosine_fusion.1
  25.6 79.2 %reduce-scatter.3.cloned.1.call-done = f32[16,1280]{1,0:T(8,128)} async-done(((f32[256,1280]{1,0:T(8,128)}), f32[16,1280]{1,0:T(8,128)}) %reduce-scatter.3.cloned.1.call-update) | async-done | bytes 81936 | tf_op jit(solution)/shard_map/reduce_scatter | solution.py:62
  104.8 0.7 slice.36
  105.6 0.1 fusion.30
  105.7 0.8 slice_bitcast_fusion
  106.6 0.1 subtract_convert_fusion
  106.7 0.2 fusion.25
  106.9 1.7 fusion.33
  108.7 0.3 fusion.2
  109.0 23.3 %all_gather.13 = bf16[256,1024]{1,0:T(8,128)(2,1)S(1)} all-gather(bf16[16,1024]{1,0:T(8,128)(2,1)S(1)} %bitcast.51), channel_id=1, replica_groups=mesh['stream'=2,'dp'=16,'tensor'=8] {'dp'}, dimensions={0}, use_global_device_ids=true | all-gather | bytes 557056 | tf_op jit(solution)/shard_map/all_gather | solution.py:113
  132.3 1.2 fusion.34
  133.6 32.9 %reduce-scatter.5.cloned.1.call-done = f32[32,512]{1,0:T(8,128)} async-done(((f32[256,512]{1,0:T(8,128)}), f32[32,512]{1,0:T(8,128)}) %reduce-scatter.5.cloned.1.call-update) | async-done | bytes 65552 | tf_op jit(solution)/shard_map/reduce_scatter | solution.py:117
  166.5 1.0 fusion.11
  167.5 40.3 %psum.21 = f32[32]{0:T(128)S(1)} all-reduce(f32[32]{0:T(128)S(1)} %fusion.11), channel_id=1, replica_groups=mesh['stream'=2,'dp'=16,'tensor'=8] {'dp'}, use_global_device_ids=true, to_apply=%region_4.5 | all-reduce | flops 32 | bytes 256 | tf_op jit(solution)/shard_map/psum | solution.py:120
  207.8 0.9 fusion.13
  208.7 15.3 %all_gather.14 = bf16[256,512]{1,0:T(8,128)(2,1)} all-gather(bf16[32,512]{1,0:T(8,128)(2,1)S(1)} %fusion.13), channel_id=1, replica_groups=mesh['stream'=2,'dp'=16,'tensor'=8] {'tensor'}, dimensions={0}, use_global_device_ids=true | all-gather | bytes 294912 | tf_op jit(solution)/shard_map/all_gather | solution.py:123
  224.1 0.1 dynamic_slice.14
  224.2 58.3 %all-gather.3.cloned.1.call-done = bf16[256,8192]{1,0:T(8,128)(2,1)} async-done(((bf16[256,512]{1,0:T(8,128)(2,1)}), bf16[256,8192]{1,0:T(8,128)(2,1)}) %all-gather.3.cloned.1.call-update) | async-done | bytes 4194320 | tf_op jit(solution)/shard_map/all_gather | solution.py:125
  282.5 7.0 %fusion.35 = f32[256,512]{1,0:T(8,128)S(1)} fusion(bf16[256,8192]{1,0:T(8,128)(2,1)} %all-gather.3.cloned.1.call-done, bf16[8192,512]{1,0:T(8,128)(2,1)} %param.21), kind=kOutput, calls=%fused_computation.66 | convolution fusion | flops 2147483648 | bytes 13107200 | tf_op jit(solution)/shard_map/dot_general | solution.py:124
  289.5 0.3 collective-permute-start
  289.8 4.7 %convert_reduce_fusion = f32[128,512]{1,0:T(8,128)S(1)} fusion(s32[512]{0:T(512)S(1)} %iota_add_fusion, s32[128,128]{1,0:T(8,128)S(1)} %constant_dynamic-slice_fusion), kind=kLoop, calls=%fused_computation | loop fusion | flops 25100288 | bytes 329728 | tf_op jit(solution)/shard_map/reduce_sum | solution.py:38
  294.4 11.4 %collective-permute-done = f32[128,512]{1,0:T(8,128)S(1)} collective-permute-done((f32[128,512]{1,0:T(8,128)S(1)}, f32[128,512]{1,0:T(8,128)S(1)}, u32[]{:S(2)}, u32[]{:S(2)}) %collective-permute-start) | collective-permute-done | bytes 262176 | tf_op jit(solution)/shard_map/ppermute | solution.py:16
  305.8 0.2 exponential_reduce_fusion
  306.0 13.6 %psum.22 = f32[128]{0:T(128)S(1)} all-reduce(f32[128]{0:T(128)S(1)} %get-tuple-element.5), channel_id=1, replica_groups=mesh['stream'=2,'dp'=16,'tensor'=8] {'tensor'}, use_global_device_ids=true, to_apply=%region_7.8 | all-reduce | flops 128 | bytes 1024 | tf_op jit(solution)/shard_map/psum | solution.py:143
  319.6 38.1 %psum.23 = f32[128]{0:T(128)S(1)} all-reduce(f32[128]{0:T(128)S(1)} %psum.22), channel_id=1, replica_groups=mesh['stream'=2,'dp'=16,'tensor'=8] {'dp'}, use_global_device_ids=true, to_apply=%region_8.9 | all-reduce | flops 128 | bytes 1024 | tf_op jit(solution)/shard_map/psum | solution.py:143
  357.7 0.8 broadcast_subtract_fusion
  (34 shorter events, 0.4 us)
Async XLA Ops:
  6.5 14.6 %copy-start = (bf16[512,1024]{1,0:T(8,128)(2,1)S(1)}, bf16[512,1024]{1,0:T(8,128)(2,1)}, u32[]{:S(2)}) copy-start(bf16[512,1024]{1,0:T(8,128)(2,1)} %param.17) | copy-start | bytes 3145732
  6.5 160.0 %copy-start.3 = (bf16[1,32,512]{2,1,0:T(8,128)(2,1)S(1)}, bf16[1,32,512]{2,1,0:T(8,128)(2,1)}, u32[]{:S(2)}) copy-start(bf16[1,32,512]{2,1,0:T(8,128)(2,1)} %param.11) | copy-start | bytes 98308
  6.5 102.2 %copy-start.1 = (bf16[1,16,1,256,128]{4,3,2,1,0:T(8,128)(2,1)S(1)}, bf16[1,16,1,256,128]{4,3,2,1,0:T(8,128)(2,1)}, u32[]{:S(2)}) copy-start(bf16[1,16,1,256,128]{4,3,2,1,0:T(8,128)(2,1)} %param.13) | copy-start | bytes 3145732
  6.5 125.8 %copy-start.2 = (bf16[1024,512]{1,0:T(8,128)(2,1)S(1)}, bf16[1024,512]{1,0:T(8,128)(2,1)}, u32[]{:S(2)}) copy-start(bf16[1024,512]{1,0:T(8,128)(2,1)} %param.19) | copy-start | bytes 3145732
  6.5 127.1 %copy-start.5 = (bf16[512]{0:T(512)(128)(2,1)S(1)}, bf16[512]{0:T(512)(128)(2,1)}, u32[]{:S(2)}) copy-start(bf16[512]{0:T(512)(128)(2,1)} %param.20) | copy-start | bytes 3076
  6.5 217.5 %copy-start.6 = (f32[256]{0:T(256)S(1)}, f32[256]{0:T(256)}, u32[]{:S(2)}) copy-start(f32[256]{0:T(256)} %param.16) | copy-start | bytes 3076
  6.6 217.6 %copy-start.4 = (s32[256,128]{1,0:T(8,128)S(1)}, s32[256,128]{1,0:T(8,128)}, u32[]{:S(2)}) copy-start(s32[256,128]{1,0:T(8,128)} %param.15) | copy-start | bytes 393220
  6.6 98.2 %reduce-scatter.3.cloned.1.call-start = ((), (), s32[]{:S(2)}) async-start(), calls=%async_computation.2 | async-start | bytes 1392640 | tf_op jit(solution)/shard_map/reduce_scatter | solution.py:62
  24.0 142.5 %reduce-scatter.5.cloned.1.call-start = ((), (), s32[]{:S(2)}) async-start(), calls=%async_computation.3 | async-start | bytes 589824 | tf_op jit(solution)/shard_map/reduce_scatter | solution.py:117
  133.6 148.9 %all-gather.3.cloned.1.call-start = ((), (), s32[]{:S(2)}) async-start(), calls=%async_computation.4 | async-start | bytes 4456448 | tf_op jit(solution)/shard_map/all_gather | solution.py:125
  289.5 16.3 %collective-permute-start = (f32[128,512]{1,0:T(8,128)S(1)}, f32[128,512]{1,0:T(8,128)S(1)}, u32[]{:S(2)}, u32[]{:S(2)}) collective-permute-start(f32[128,512]{1,0:T(8,128)S(1)} %constant_dynamic-slice_fusion.1), channel_id=1, source_target_pairs={{0,128},{128,0},{1,129},{129,1},{2,130},{130,2},{3,131},{131,3},{4... | collective-permute-start | bytes 786440 | tf_op jit(solution)/shard_map/ppermute | solution.py:16
Sparse Core Ops, SparseCore 0:
  24.1 80.6 reduce-scatter.2
  133.7 32.7 reduce-scatter.4
  224.2 58.2 all-gather.2
